TPU v7x, 32 devices: a whole 2x2x4 slice. The times are simulated.
32 devices in a mesh: ctx: 8 (over y, x, core), ch: 4 (over z).
Axes of the slice: x: 2, y: 2, z: 4, core: 2. Of those that a mesh axis runs over, the one named last changes fastest.
Arguments:
- tokens_in: bfloat16 [1792, 4096], P('ctx', 'ch'), may hold values from -6 to 6
- norm_gain: bfloat16 [4096], P('ch'), may hold values from 0.5 to 1.5
- w_qkv: bfloat16 [4096, 3, 2048], P('ch'), may hold values from -0.09375 to 0.09375
- short_filter: float32 [3, 3, 2048], P(None, None, 'ch'), may hold values from -3.5 to 3.5
- residue: float32 [2048, 16], P('ch'), may hold values from -1.5 to 1.5
- decay_rate: float32 [2048, 16], P('ch'), may hold values from 0.00027901787 to 0.025
- skip_bias: float32 [2048], P('ch'), may hold values from -4 to 4
- w_out: bfloat16 [2048, 4096], P(None, 'ch'), may hold values from -0.125 to 0.125
Outputs:
- mixed_out: bfloat16 [1792, 4096], P('ctx', 'ch')
All inputs are finite; a program needn't handle non-finite values.
Results may differ from a plain program's by a relative error of at most 0.011.
Values may be sent and summed in bfloat16 or wider, within the bound.
A program may use at most 128 MiB of HBM per device.

v0:
```python
import functools

import jax
import jax.numpy as jnp
from jax import lax
from jax.experimental import pallas as pl
from jax.experimental.pallas import tpu as pltpu
from jax.sharding import PartitionSpec as P

D = 4096
SHORT = 3
ORDER = 16
LANES = 128
SUB = 32
HALO = 16
MESH = pl.DeviceIdType.MESH


def kernel(
    n_ctx, n_ch, rows, chunks,
    tok_ref, gain_ref, w_hbm, sf_ref, res_ref, dec_ref, skip_ref, wout_hbm, out_ref,
    scaled, wbuf, woutbuf, up_send, up_recv, dn_send, dn_recv,
    sq_send, sq_recv, square, scale_ref, p_sf, p_res, p_dec, p_skip,
    fpad, halo_send, halo_recv, st_send, st_recv, local_st, gz, gated_ref, query_ref, local_y, gobuf,
    w_sem, wout_sem, up_ss, up_rs, dn_ss, dn_rs, sq_ss, sq_rs, p_ss, p_rs,
    h_ss, h_rs, st_ss, st_rs, gu_ss, gu_rs, gd_ss, gd_rs,
):
    me = lax.axis_index("ctx")
    z = lax.axis_index("ch")
    last = n_ch - 1
    width = 3 * LANES
    half = chunks * LANES
    blocks = rows // SUB
    dev_ch = sf_ref.shape[2]
    is_end = (z == 0) | (z == last)

    def weight_copies(index):
        start = pl.multiple_of(index * LANES, LANES)
        return [
            pltpu.make_async_copy(
                w_hbm.at[s, :, pl.ds(start, LANES)],
                wbuf.at[index, :, pl.ds(s * LANES, LANES)],
                w_sem.at[index, s],
            )
            for s in range(3)
        ]

    def start_weights(j, _):
        for copy in weight_copies(chunks + j):
            copy.start()
        for copy in weight_copies(j):
            copy.start()
        return 0

    lax.fori_loop(0, chunks, start_weights, 0)
    wout_copy = pltpu.make_async_copy(wout_hbm, woutbuf, wout_sem)
    wout_copy.start()

    barrier = pltpu.get_barrier_semaphore()
    for k in range(1, n_ch):
        pl.semaphore_signal(
            barrier, inc=1, device_id={"ch": lax.rem(z + k, n_ch)}, device_id_type=MESH
        )

    def greet(k, _):
        pl.semaphore_signal(
            barrier, inc=1, device_id={"ctx": lax.rem(me + k, n_ctx)}, device_id_type=MESH
        )
        return 0

    lax.fori_loop(1, n_ctx, greet, 0)

    wide = tok_ref[...].astype(jnp.float32)
    scaled[...] = (wide * gain_ref[...].astype(jnp.float32)).astype(jnp.bfloat16)
    wide = wide * wide
    folded = wide[:, :LANES]
    for k in range(1, wide.shape[1] // LANES):
        folded = folded + wide[:, k * LANES : (k + 1) * LANES]
    square[...] = jnp.zeros_like(square)
    square[pl.ds(0, rows), :] = folded
    turned = jnp.sum(square[...].T, axis=0, keepdims=True)
    sq_send[...] = jnp.broadcast_to(turned, sq_send.shape)

    pl.semaphore_wait(barrier, n_ch - 1 + n_ctx - 1)

    def sq_copy(k):
        return pltpu.make_async_remote_copy(
            src_ref=sq_send, dst_ref=sq_recv.at[k - 1], send_sem=sq_ss.at[k - 1],
            recv_sem=sq_rs.at[k - 1], device_id={"ch": lax.rem(z + k, n_ch)}, device_id_type=MESH,
        )

    for k in range(1, n_ch):
        sq_copy(k).start()
    own_half = lax.rem(z, 2)
    partner = z + 1 - 2 * own_half
    p_copies = [
        pltpu.make_async_remote_copy(
            src_ref=src, dst_ref=dst.at[own_half], send_sem=p_ss.at[i], recv_sem=p_rs.at[i],
            device_id={"ch": partner}, device_id_type=MESH,
        )
        for i, (src, dst) in enumerate(
            ((sf_ref, p_sf), (res_ref, p_res), (dec_ref, p_dec), (skip_ref, p_skip))
        )
    ]
    for copy in p_copies:
        copy.start()
    p_sf[own_half] = sf_ref[...]
    p_res[own_half] = res_ref[...]
    p_dec[own_half] = dec_ref[...]
    p_skip[own_half] = skip_ref[...]

    def partial(index):
        for copy in weight_copies(index):
            copy.wait()
        return jnp.dot(scaled[...], wbuf[index], preferred_element_type=jnp.float32)

    def up_copy(j):
        return pltpu.make_async_remote_copy(
            src_ref=up_send.at[j], dst_ref=up_recv.at[j], send_sem=up_ss.at[j],
            recv_sem=up_rs.at[j], device_id={"ch": jnp.minimum(z + 1, last)}, device_id_type=MESH,
        )

    def dn_copy(j):
        return pltpu.make_async_remote_copy(
            src_ref=dn_send.at[j], dst_ref=dn_recv.at[j], send_sem=dn_ss.at[j],
            recv_sem=dn_rs.at[j], device_id={"ch": jnp.maximum(z - 1, 0)}, device_id_type=MESH,
        )

    def halo_copy(j):
        return pltpu.make_async_remote_copy(
            src_ref=halo_send.at[j], dst_ref=halo_recv.at[j], send_sem=h_ss.at[j],
            recv_sem=h_rs.at[j], device_id={"ctx": jnp.minimum(me + 1, n_ctx - 1)}, device_id_type=MESH,
        )

    def state_copy(j, k):
        return pltpu.make_async_remote_copy(
            src_ref=st_send.at[j], dst_ref=st_recv.at[j, k - 1], send_sem=st_ss.at[j],
            recv_sem=st_rs.at[j], device_id={"ctx": lax.rem(me + k, n_ctx)}, device_id_type=MESH,
        )

    def gu_copy(j):
        piece = gobuf.at[:, pl.ds(pl.multiple_of(j * LANES, LANES), LANES)]
        return pltpu.make_async_remote_copy(
            src_ref=piece, dst_ref=piece, send_sem=gu_ss.at[j],
            recv_sem=gu_rs.at[j], device_id={"ch": jnp.minimum(z + 1, last)}, device_id_type=MESH,
        )

    def gd_copy(j):
        piece = gobuf.at[:, pl.ds(pl.multiple_of(half + j * LANES, LANES), LANES)]
        return pltpu.make_async_remote_copy(
            src_ref=piece, dst_ref=piece, send_sem=gd_ss.at[j],
            recv_sem=gd_rs.at[j], device_id={"ch": jnp.maximum(z - 1, 0)}, device_id_type=MESH,
        )

    def finish_scale():
        total = sq_send[...]
        for k in range(1, n_ch):
            total = total + sq_recv[k - 1]
        mean_sq = jnp.broadcast_to(total[0:1] * (1.0 / D), (LANES, total.shape[1])).T
        scale_ref[...] = lax.rsqrt(mean_sq + 1e-06)[:rows]

    def stage_a(j, proj):
        scale = scale_ref[...]
        for s in range(3):
            feats = (proj[:, s * LANES : (s + 1) * LANES] * scale).astype(jnp.bfloat16)
            fpad[j, s, pl.ds(HALO, rows), :] = feats.astype(jnp.float32)
            halo_send[j, s] = feats[rows - HALO :]

        @pl.when(me < n_ctx - 1)
        def _():
            halo_copy(j).start()

    def lane_of(j):
        per = dev_ch // LANES
        return j // per, pl.ds(pl.multiple_of(lax.rem(j, per) * LANES, LANES), LANES)

    def stage_b(j):
        side, lanes = lane_of(j)

        @pl.when(me > 0)
        def _():
            halo_copy(j).wait_recv()
            for s in range(3):
                fpad[j, s, pl.ds(0, HALO), :] = halo_recv[j, s].astype(jnp.float32)

        @pl.when(me == 0)
        def _():
            for s in range(3):
                fpad[j, s, pl.ds(0, HALO), :] = jnp.zeros((HALO, LANES), jnp.float32)

        def featurized(s):
            total = p_sf[side, 0, pl.ds(s, 1), lanes] * fpad[j, s, pl.ds(HALO, rows), :]
            for lag in range(1, SHORT):
                tap = p_sf[side, lag, pl.ds(s, 1), lanes]
                total = total + tap * fpad[j, s, pl.ds(HALO - lag, rows), :]
            return total

        query_ref[j] = featurized(0)
        gated = (featurized(1) * featurized(2)).astype(jnp.bfloat16).astype(jnp.float32)
        gated_ref[j] = gated
        for b in range(blocks):
            gz[b, pl.ds(SUB, SUB), :] = gated[b * SUB : (b + 1) * SUB]
        decay = p_dec[side, :, lanes]
        weight = p_res[side, :, lanes] * jnp.sqrt(2.0 * decay)
        lag_rows = lax.broadcasted_iota(jnp.int32, (SUB, LANES), 0).astype(jnp.float32)
        taps = jnp.zeros((SUB, LANES), jnp.float32)
        for r in range(ORDER):
            taps = taps + weight[r : r + 1] * jnp.exp(-decay[r : r + 1] * lag_rows)
        falls = [jnp.exp(decay * (-float(SUB - 1 - u))) for u in range(SUB)]
        jump = jnp.exp(decay * (-float(SUB)))

        def block(b, state):
            local_st[j, b] = state
            total = taps[0:1] * gz[b, pl.ds(SUB, SUB), :]
            for k in range(1, SUB):
                total = total + taps[k : k + 1] * gz[b, pl.ds(SUB - k, SUB), :]
            local_y[j, b] = total
            state = state * jump
            for u in range(SUB):
                state = state + falls[u] * gz[b, pl.ds(SUB + u, 1), :]
            return state

        state = lax.fori_loop(0, blocks, block, jnp.zeros((ORDER, LANES), jnp.float32))
        st_send[j] = state

        def send(k, _):
            state_copy(j, k).start()
            return 0

        lax.fori_loop(1, n_ctx, send, 0)

    def stage_c(j):
        side, lanes = lane_of(j)
        pltpu.make_async_copy(st_recv.at[j], st_recv.at[j], st_rs.at[j]).wait()
        decay = p_dec[side, :, lanes]
        weight = p_res[side, :, lanes] * jnp.sqrt(2.0 * decay)

        def gather(k, state):
            far = jnp.full((ORDER, LANES), (k - 1) * rows, jnp.int32).astype(jnp.float32)
            term = jnp.exp(-decay * far) * st_recv[j, k - 1]
            return state + jnp.where(jnp.full((ORDER, LANES), k, jnp.int32) <= me, term, 0.0)

        incoming = lax.fori_loop(1, n_ctx, gather, jnp.zeros((ORDER, LANES), jnp.float32))
        lag_rows = lax.broadcasted_iota(jnp.int32, (SUB, LANES), 0).astype(jnp.float32) + 1.0
        tables = [
            weight[r : r + 1] * jnp.exp(-decay[r : r + 1] * lag_rows) for r in range(ORDER)
        ]
        jump = jnp.exp(decay * (-float(SUB)))
        skip = p_skip[side, :, lanes]
        start = pl.multiple_of(jnp.where(z == 0, 0, half) + j * LANES, LANES)
        for b in range(blocks):
            state = local_st[j, b] + incoming
            total = local_y[j, b]
            for r in range(ORDER):
                total = total + tables[r] * state[r : r + 1]
            conv = total.astype(jnp.bfloat16).astype(jnp.float32)
            span = pl.ds(b * SUB, SUB)
            mixed = query_ref[j, span, :] * (conv + skip * gated_ref[j, span, :])
            gobuf[span, pl.ds(start, LANES)] = mixed.astype(jnp.bfloat16)
            incoming = incoming * jump

        @pl.when(z == 0)
        def _():
            gu_copy(j).start()

        @pl.when(z == last)
        def _():
            gd_copy(j).start()

    gz[...] = jnp.zeros_like(gz)

    def step(s, _):
        cu = s - z
        cd = s - (last - z)
        fin = s - last

        @pl.when((z < last) & (cu >= 0) & (cu < chunks))
        def _():
            total = partial(chunks + cu)

            @pl.when(z == 0)
            def _():
                up_send[cu] = total.astype(jnp.bfloat16)

            @pl.when(z > 0)
            def _():
                up_copy(cu).wait_recv()
                up_send[cu] = (total + up_recv[cu].astype(jnp.float32)).astype(jnp.bfloat16)

            up_copy(cu).start()

        @pl.when((z > 0) & (cd >= 0) & (cd < chunks))
        def _():
            total = partial(cd)

            @pl.when(z == last)
            def _():
                dn_send[cd] = total.astype(jnp.bfloat16)

            @pl.when(z < last)
            def _():
                dn_copy(cd).wait_recv()
                dn_send[cd] = (total + dn_recv[cd].astype(jnp.float32)).astype(jnp.bfloat16)

            dn_copy(cd).start()

        @pl.when(s == last)
        def _():
            for k in range(1, n_ch):
                sq_copy(k).wait()
            for copy in p_copies:
                copy.wait()
            finish_scale()

        @pl.when(is_end & (fin >= 2) & (fin < chunks + 2))
        def _():
            stage_c(fin - 2)

        @pl.when(is_end & (fin >= 1) & (fin < chunks + 1))
        def _():
            stage_b(fin - 1)

        @pl.when((z == 0) & (fin >= 0) & (fin < chunks))
        def _():
            total = partial(fin)
            dn_copy(fin).wait_recv()
            stage_a(fin, total + dn_recv[fin].astype(jnp.float32))

        @pl.when((z == last) & (fin >= 0) & (fin < chunks))
        def _():
            total = partial(chunks + fin)
            up_copy(fin).wait_recv()
            stage_a(fin, total + up_recv[fin].astype(jnp.float32))

        fu = s - (last + 2) - 2 * z
        fd = s - (last + 2) - 2 * (last - z)

        @pl.when((z > 0) & (z < last) & (fu >= 0) & (fu < chunks))
        def _():
            gu_copy(fu).wait_recv()
            gu_copy(fu).start()

        @pl.when((z > 0) & (z < last) & (fd >= 0) & (fd < chunks))
        def _():
            gd_copy(fd).wait_recv()
            gd_copy(fd).start()

        return 0

    lax.fori_loop(0, chunks + last + 2 + 2 * (last - 1), step, 0)

    wout_copy.wait()

    def finish(j, _):
        @pl.when(z < last)
        def _():
            up_copy(j).wait_send()
            gu_copy(j).wait_send()

        @pl.when(z > 0)
        def _():
            dn_copy(j).wait_send()
            gd_copy(j).wait_send()

        @pl.when(z == last)
        def _():
            gu_copy(j).wait_recv()

        @pl.when(z == 0)
        def _():
            gd_copy(j).wait_recv()

        @pl.when(is_end & (me < n_ctx - 1))
        def _():
            halo_copy(j).wait_send()

        @pl.when(is_end)
        def _():
            pltpu.make_async_copy(st_recv.at[j], st_recv.at[j], st_ss.at[j]).wait()

        return 0

    lax.fori_loop(0, chunks, finish, 0)

    tile = 256

    def project(t, _):
        cols = pl.ds(pl.multiple_of(t * tile, tile), tile)
        out_ref[:, cols] = jnp.dot(
            gobuf[...], woutbuf[:, cols], preferred_element_type=jnp.float32
        ).astype(jnp.bfloat16)
        return 0

    lax.fori_loop(0, out_ref.shape[1] // tile, project, 0)


def local(tokens_in, norm_gain, w_qkv, short_filter, residue, decay_rate, skip_bias, w_out):
    rows, feat = tokens_in.shape
    slab = w_qkv.shape[2]
    dev_ch = short_filter.shape[2]
    n_ctx = lax.axis_size("ctx")
    n_ch = lax.axis_size("ch")
    chunks = slab // 2 // LANES
    width = 3 * LANES
    padded = -(-rows // LANES) * LANES
    blocks = rows // SUB
    vmem = pl.BlockSpec(memory_space=pltpu.VMEM)
    hbm = pl.BlockSpec(memory_space=pl.ANY)
    bf, f32 = jnp.bfloat16, jnp.float32
    dma = pltpu.SemaphoreType.DMA
    V = pltpu.VMEM
    return pl.pallas_call(
        functools.partial(kernel, n_ctx, n_ch, rows, chunks),
        out_shape=jax.ShapeDtypeStruct((rows, w_out.shape[1]), bf),
        in_specs=[vmem, vmem, hbm, vmem, vmem, vmem, vmem, hbm],
        out_specs=vmem,
        scratch_shapes=[
            V((rows, feat), bf), V((2 * chunks, feat, width), bf), V(w_out.shape, bf),
            V((chunks, rows, width), bf), V((chunks, rows, width), bf),
            V((chunks, rows, width), bf), V((chunks, rows, width), bf),
            V((8, padded), f32), V((n_ch - 1, 8, padded), f32), V((padded, LANES), f32),
            V((rows, LANES), f32),
            V((2, SHORT, 3, dev_ch), f32), V((2, ORDER, dev_ch), f32), V((2, ORDER, dev_ch), f32),
            V((2, 1, dev_ch), f32),
            V((chunks, 3, HALO + rows, LANES), f32),
            V((chunks, 3, HALO, LANES), bf), V((chunks, 3, HALO, LANES), bf),
            V((chunks, ORDER, LANES), f32), V((chunks, n_ctx - 1, ORDER, LANES), f32),
            V((chunks, blocks, ORDER, LANES), f32), V((blocks, 2 * SUB, LANES), f32),
            V((chunks, rows, LANES), f32), V((chunks, rows, LANES), f32),
            V((chunks, blocks, SUB, LANES), f32), V((rows, slab), bf),
            dma((2 * chunks, 3)), dma, dma((chunks,)), dma((chunks,)), dma((chunks,)), dma((chunks,)),
            dma((n_ch - 1,)), dma((n_ch - 1,)), dma((4,)), dma((4,)),
            dma((chunks,)), dma((chunks,)), dma((chunks,)), dma((chunks,)),
            dma((chunks,)), dma((chunks,)), dma((chunks,)), dma((chunks,)),
        ],
        compiler_params=pltpu.CompilerParams(
            collective_id=0, has_side_effects=True, vmem_limit_bytes=56 * 2**20
        ),
        name="hyena",
    )(
        tokens_in, norm_gain.reshape(1, feat), jnp.transpose(w_qkv, (1, 0, 2)), short_filter,
        residue.T, decay_rate.T, skip_bias.reshape(1, dev_ch), w_out,
    )


def solution(mesh):
    return jax.shard_map(
        local,
        mesh=mesh,
        in_specs=(
            P("ctx", "ch"),
            P("ch"),
            P("ch", None, None),
            P(None, None, "ch"),
            P("ch", None),
            P("ch", None),
            P("ch"),
            P(None, "ch"),
        ),
        out_specs=P("ctx", "ch"),
        check_vma=False,
    )
```

profile of v0, /device:TPU:0, one launch (start us, length us, event | category | flops | bytes accessed | tf_op | source)
XLA Modules:
  0.0 81.7 jit_solution(7138625006891153187)
XLA Ops:
  0.0 1.3 %reshape.6.gain_ref = bf16[1,1024]{1,0:T(2,128)(2,1)} reshape(bf16[1024]{0:T(1024)(128)(2,1)} %param.9) | data formatting | bytes 4096 | tf_op jit(solution)/shard_map/reshape | solution.py:441
  1.3 78.6 %hyena.1 = bf16[224,1024]{1,0:T(8,128)(2,1)} custom-call(bf16[224,1024]{1,0:T(8,128)(2,1)} %tok_ref.1, bf16[1,1024]{1,0:T(2,128)(2,1)} %reshape.6.gain_ref, bf16[3,1024,2048]{2,1,0:T(8,128)(2,1)} %bitcast.4, f32[3,3,512]{2,1,0:T(4,128)} %sf_ref.1, f32[16,512]{1,0:T(8,128)} %bitcast.5, f32[16,512]{1,0:T(8,128)} %bitcast.6, f32[1,512]{1,0:T(1,128)} %bitcast.7, ...), custom_call_target="tpu_custom_call" | custom-call | tf_op jit(solution)/shard_map/hyena/pallas_call | solution.py:412
  79.9 1.8 %copy.10 = bf16[224,1024]{1,0:T(8,128)(2,1)} copy(bf16[224,1024]{1,0:T(8,128)(2,1)} %hyena.1) | data formatting | bytes 917504
where the time goes:
time: 81.9 us; the launch traced here: 81.7 us
  Pallas kernels  78.6 us (96%)
  local copies, waits for them, and re-layouts  3.09 us (4%)
    pallas_call x1, Pallas kernels, local(): pl.pallas_call(functools.partial(kernel, n_ctx, n_ch, rows, chunks), out_...  78.6 us
    unnamed x1, local copies, waits for them, and re-layouts  1.82 us

commit v1 on v0

--- a/solution.py
+++ b/solution.py
@@ -12,6 +12,8 @@
 ORDER = 16
 LANES = 128
 SUB = 32
+LEAD = 8
+PIECES = 2
 HALO = 16
 MESH = pl.DeviceIdType.MESH
 
@@ -30,9 +32,11 @@
     last = n_ch - 1
     width = 3 * LANES
     half = chunks * LANES
+    piece_rows = rows // PIECES
     blocks = rows // SUB
     dev_ch = sf_ref.shape[2]
     is_end = (z == 0) | (z == last)
+    is_mid = (z > 0) & (z < last)
 
     def weight_copies(index):
         start = pl.multiple_of(index * LANES, LANES)
@@ -71,7 +75,7 @@
     lax.fori_loop(1, n_ctx, greet, 0)
 
     wide = tok_ref[...].astype(jnp.float32)
-    scaled[...] = (wide * gain_ref[...].astype(jnp.float32)).astype(jnp.bfloat16)
+    scaled[...] = (wide * gain_ref[...].astype(jnp.float32).reshape(1, -1)).astype(jnp.bfloat16)
     wide = wide * wide
     folded = wide[:, :LANES]
     for k in range(1, wide.shape[1] // LANES):
@@ -114,16 +118,18 @@
             copy.wait()
         return jnp.dot(scaled[...], wbuf[index], preferred_element_type=jnp.float32)
 
-    def up_copy(j):
-        return pltpu.make_async_remote_copy(
-            src_ref=up_send.at[j], dst_ref=up_recv.at[j], send_sem=up_ss.at[j],
-            recv_sem=up_rs.at[j], device_id={"ch": jnp.minimum(z + 1, last)}, device_id_type=MESH,
-        )
-
-    def dn_copy(j):
-        return pltpu.make_async_remote_copy(
-            src_ref=dn_send.at[j], dst_ref=dn_recv.at[j], send_sem=dn_ss.at[j],
-            recv_sem=dn_rs.at[j], device_id={"ch": jnp.maximum(z - 1, 0)}, device_id_type=MESH,
+    def up_copy(j, i):
+        span = pl.ds(i * piece_rows, piece_rows)
+        return pltpu.make_async_remote_copy(
+            src_ref=up_send.at[j, span], dst_ref=up_recv.at[j, span], send_sem=up_ss.at[j, i],
+            recv_sem=up_rs.at[j, i], device_id={"ch": jnp.minimum(z + 1, last)}, device_id_type=MESH,
+        )
+
+    def dn_copy(j, i):
+        span = pl.ds(i * piece_rows, piece_rows)
+        return pltpu.make_async_remote_copy(
+            src_ref=dn_send.at[j, span], dst_ref=dn_recv.at[j, span], send_sem=dn_ss.at[j, i],
+            recv_sem=dn_rs.at[j, i], device_id={"ch": jnp.maximum(z - 1, 0)}, device_id_type=MESH,
         )
 
     def halo_copy(j):
@@ -221,23 +227,30 @@
             return state
 
         state = lax.fori_loop(0, blocks, block, jnp.zeros((ORDER, LANES), jnp.float32))
-        st_send[j] = state
+        st_send[j // 2, lax.rem(j, 2)] = state
 
         def send(k, _):
-            state_copy(j, k).start()
+            state_copy(j // 2, k).start()
             return 0
 
-        lax.fori_loop(1, n_ctx, send, 0)
+        @pl.when(lax.rem(j, 2) == 1)
+        def _():
+            lax.fori_loop(1, n_ctx, send, 0)
 
     def stage_c(j):
         side, lanes = lane_of(j)
-        pltpu.make_async_copy(st_recv.at[j], st_recv.at[j], st_rs.at[j]).wait()
+        pair = j // 2
+
+        @pl.when(lax.rem(j, 2) == 0)
+        def _():
+            pltpu.make_async_copy(st_recv.at[pair], st_recv.at[pair], st_rs.at[pair]).wait()
+
         decay = p_dec[side, :, lanes]
         weight = p_res[side, :, lanes] * jnp.sqrt(2.0 * decay)
 
         def gather(k, state):
             far = jnp.full((ORDER, LANES), (k - 1) * rows, jnp.int32).astype(jnp.float32)
-            term = jnp.exp(-decay * far) * st_recv[j, k - 1]
+            term = jnp.exp(-decay * far) * st_recv[pair, k - 1, lax.rem(j, 2)]
             return state + jnp.where(jnp.full((ORDER, LANES), k, jnp.int32) <= me, term, 0.0)
 
         incoming = lax.fori_loop(1, n_ctx, gather, jnp.zeros((ORDER, LANES), jnp.float32))
@@ -267,54 +280,76 @@
         def _():
             gd_copy(j).start()
 
+    def lead_up(j, _):
+        up_send[j] = partial(chunks + j).astype(jnp.bfloat16)
+        for i in range(PIECES):
+            up_copy(j, i).start()
+        return 0
+
+    def lead_dn(j, _):
+        dn_send[j] = partial(j).astype(jnp.bfloat16)
+        for i in range(PIECES):
+            dn_copy(j, i).start()
+        return 0
+
+    @pl.when(z == 0)
+    def _():
+        lax.fori_loop(0, LEAD, lead_up, 0)
+
+    @pl.when(z == last)
+    def _():
+        lax.fori_loop(0, LEAD, lead_dn, 0)
+
     gz[...] = jnp.zeros_like(gz)
+    def settle():
+        for k in range(1, n_ch):
+            sq_copy(k).wait()
+        for copy in p_copies:
+            copy.wait()
+
+    @pl.when(is_end)
+    def _():
+        settle()
+        finish_scale()
 
     def step(s, _):
-        cu = s - z
-        cd = s - (last - z)
-        fin = s - last
-
-        @pl.when((z < last) & (cu >= 0) & (cu < chunks))
+        cu = s + 1 - z
+        cd = s + 1 - (last - z)
+        fin = s
+
+        @pl.when((z == 0) & (s + LEAD < chunks))
+        def _():
+            lead_up(s + LEAD, 0)
+
+        @pl.when((z == last) & (s + LEAD < chunks))
+        def _():
+            lead_dn(s + LEAD, 0)
+
+        @pl.when(is_mid & (cu >= 0) & (cu < chunks))
         def _():
             total = partial(chunks + cu)
-
-            @pl.when(z == 0)
-            def _():
-                up_send[cu] = total.astype(jnp.bfloat16)
-
-            @pl.when(z > 0)
-            def _():
-                up_copy(cu).wait_recv()
-                up_send[cu] = (total + up_recv[cu].astype(jnp.float32)).astype(jnp.bfloat16)
-
-            up_copy(cu).start()
-
-        @pl.when((z > 0) & (cd >= 0) & (cd < chunks))
+            for i in range(PIECES):
+                span = pl.ds(i * piece_rows, piece_rows)
+                up_copy(cu, i).wait_recv()
+                mine = total[i * piece_rows : (i + 1) * piece_rows]
+                theirs = up_recv[cu, span, :].astype(jnp.float32)
+                up_send[cu, span, :] = (mine + theirs).astype(jnp.bfloat16)
+                up_copy(cu, i).start()
+
+        @pl.when(is_mid & (cd >= 0) & (cd < chunks))
         def _():
             total = partial(cd)
-
-            @pl.when(z == last)
-            def _():
-                dn_send[cd] = total.astype(jnp.bfloat16)
-
-            @pl.when(z < last)
-            def _():
-                dn_copy(cd).wait_recv()
-                dn_send[cd] = (total + dn_recv[cd].astype(jnp.float32)).astype(jnp.bfloat16)
-
-            dn_copy(cd).start()
-
-        @pl.when(s == last)
-        def _():
-            for k in range(1, n_ch):
-                sq_copy(k).wait()
-            for copy in p_copies:
-                copy.wait()
-            finish_scale()
-
-        @pl.when(is_end & (fin >= 2) & (fin < chunks + 2))
-        def _():
-            stage_c(fin - 2)
+            for i in range(PIECES):
+                span = pl.ds(i * piece_rows, piece_rows)
+                dn_copy(cd, i).wait_recv()
+                mine = total[i * piece_rows : (i + 1) * piece_rows]
+                theirs = dn_recv[cd, span, :].astype(jnp.float32)
+                dn_send[cd, span, :] = (mine + theirs).astype(jnp.bfloat16)
+                dn_copy(cd, i).start()
+
+        @pl.when(is_end & (fin >= 3) & (fin < chunks + 3))
+        def _():
+            stage_c(fin - 3)
 
         @pl.when(is_end & (fin >= 1) & (fin < chunks + 1))
         def _():
@@ -323,17 +358,19 @@
         @pl.when((z == 0) & (fin >= 0) & (fin < chunks))
         def _():
             total = partial(fin)
-            dn_copy(fin).wait_recv()
+            for i in range(PIECES):
+                dn_copy(fin, i).wait_recv()
             stage_a(fin, total + dn_recv[fin].astype(jnp.float32))
 
         @pl.when((z == last) & (fin >= 0) & (fin < chunks))
         def _():
             total = partial(chunks + fin)
-            up_copy(fin).wait_recv()
+            for i in range(PIECES):
+                up_copy(fin, i).wait_recv()
             stage_a(fin, total + up_recv[fin].astype(jnp.float32))
 
-        fu = s - (last + 2) - 2 * z
-        fd = s - (last + 2) - 2 * (last - z)
+        fu = s - chunks + 3 - 2 * z
+        fd = s - chunks + 3 - 2 * (last - z)
 
         @pl.when((z > 0) & (z < last) & (fu >= 0) & (fu < chunks))
         def _():
@@ -347,19 +384,25 @@
 
         return 0
 
-    lax.fori_loop(0, chunks + last + 2 + 2 * (last - 1), step, 0)
+    lax.fori_loop(0, 2 * chunks - 3 + 2 * (last - 1), step, 0)
+
+    @pl.when(is_mid)
+    def _():
+        settle()
 
     wout_copy.wait()
 
     def finish(j, _):
         @pl.when(z < last)
         def _():
-            up_copy(j).wait_send()
+            for i in range(PIECES):
+                up_copy(j, i).wait_send()
             gu_copy(j).wait_send()
 
         @pl.when(z > 0)
         def _():
-            dn_copy(j).wait_send()
+            for i in range(PIECES):
+                dn_copy(j, i).wait_send()
             gd_copy(j).wait_send()
 
         @pl.when(z == last)
@@ -374,7 +417,7 @@
         def _():
             halo_copy(j).wait_send()
 
-        @pl.when(is_end)
+        @pl.when(is_end & (j < chunks // 2))
         def _():
             pltpu.make_async_copy(st_recv.at[j], st_recv.at[j], st_ss.at[j]).wait()
 
@@ -424,13 +467,14 @@
             V((2, 1, dev_ch), f32),
             V((chunks, 3, HALO + rows, LANES), f32),
             V((chunks, 3, HALO, LANES), bf), V((chunks, 3, HALO, LANES), bf),
-            V((chunks, ORDER, LANES), f32), V((chunks, n_ctx - 1, ORDER, LANES), f32),
+            V((chunks // 2, 2, ORDER, LANES), f32), V((chunks // 2, n_ctx - 1, 2, ORDER, LANES), f32),
             V((chunks, blocks, ORDER, LANES), f32), V((blocks, 2 * SUB, LANES), f32),
             V((chunks, rows, LANES), f32), V((chunks, rows, LANES), f32),
             V((chunks, blocks, SUB, LANES), f32), V((rows, slab), bf),
-            dma((2 * chunks, 3)), dma, dma((chunks,)), dma((chunks,)), dma((chunks,)), dma((chunks,)),
+            dma((2 * chunks, 3)), dma, dma((chunks, PIECES)), dma((chunks, PIECES)),
+            dma((chunks, PIECES)), dma((chunks, PIECES)),
             dma((n_ch - 1,)), dma((n_ch - 1,)), dma((4,)), dma((4,)),
-            dma((chunks,)), dma((chunks,)), dma((chunks,)), dma((chunks,)),
+            dma((chunks,)), dma((chunks,)), dma((chunks // 2,)), dma((chunks // 2,)),
             dma((chunks,)), dma((chunks,)), dma((chunks,)), dma((chunks,)),
         ],
         compiler_params=pltpu.CompilerParams(
@@ -438,7 +482,7 @@
         ),
         name="hyena",
     )(
-        tokens_in, norm_gain.reshape(1, feat), jnp.transpose(w_qkv, (1, 0, 2)), short_filter,
+        tokens_in, norm_gain, jnp.transpose(w_qkv, (1, 0, 2)), short_filter,
         residue.T, decay_rate.T, skip_bias.reshape(1, dev_ch), w_out,
     )
 

time: 81.9 us -> 77.6 us (0.947)
  Pallas kernels: 78.6 us -> 75.6 us
  local copies, waits for them, and re-layouts: 3.09 us -> 1.82 us
    pallas_call x1, Pallas kernels: 78.6 us -> 75.6 us  [local(): pl.pallas_call(functools.partial(kernel, n_ctx, n_ch, rows, chunks), out_...]
    reshape x1 -> x0, local copies, waits for them, and re-layouts: 1.28 us -> none  [local(): norm_gain.reshape(1, feat)]
where the time goes in v1:
time: 77.6 us; the launch traced here: 77.4 us
  Pallas kernels  75.6 us (97%)
  local copies, waits for them, and re-layouts  1.82 us (2%)
    pallas_call x1, Pallas kernels, local(): pl.pallas_call(functools.partial(kernel, n_ctx, n_ch, rows, chunks), out_...  75.6 us
    unnamed x1, local copies, waits for them, and re-layouts  1.82 us

profile of v1, /device:TPU:0, one launch (start us, length us, event | category | flops | bytes accessed | tf_op | source)
XLA Modules:
  0.0 77.4 jit_solution(5466869982677205280)
XLA Ops:
  0.0 75.6 %hyena.1 = bf16[224,1024]{1,0:T(8,128)(2,1)} custom-call(bf16[224,1024]{1,0:T(8,128)(2,1)} %tok_ref.1, bf16[1024]{0:T(1024)(128)(2,1)} %gain_ref.1, bf16[3,1024,2048]{2,1,0:T(8,128)(2,1)} %bitcast.4, f32[3,3,512]{2,1,0:T(4,128)} %sf_ref.1, f32[16,512]{1,0:T(8,128)} %bitcast.5, f32[16,512]{1,0:T(8,128)} %bitcast.6, f32[1,512]{1,0:T(1,128)} %bitcast.7, ...), custom_call_target="tpu_custom_call" | custom-call | tf_op jit(solution)/shard_map/hyena/pallas_call | solution.py:455
  75.6 1.8 %copy.10 = bf16[224,1024]{1,0:T(8,128)(2,1)} copy(bf16[224,1024]{1,0:T(8,128)(2,1)} %hyena.1) | data formatting | bytes 917504

commit v2 on v1

--- a/solution.py
+++ b/solution.py
@@ -347,13 +347,13 @@
                 dn_send[cd, span, :] = (mine + theirs).astype(jnp.bfloat16)
                 dn_copy(cd, i).start()
 
-        @pl.when(is_end & (fin >= 3) & (fin < chunks + 3))
-        def _():
-            stage_c(fin - 3)
-
-        @pl.when(is_end & (fin >= 1) & (fin < chunks + 1))
-        def _():
-            stage_b(fin - 1)
+        @pl.when(is_end & (fin >= 5) & (fin < chunks + 5))
+        def _():
+            stage_c(fin - 5)
+
+        @pl.when(is_end & (fin >= 2) & (fin < chunks + 2))
+        def _():
+            stage_b(fin - 2)
 
         @pl.when((z == 0) & (fin >= 0) & (fin < chunks))
         def _():
@@ -369,8 +369,8 @@
                 up_copy(fin, i).wait_recv()
             stage_a(fin, total + up_recv[fin].astype(jnp.float32))
 
-        fu = s - chunks + 3 - 2 * z
-        fd = s - chunks + 3 - 2 * (last - z)
+        fu = s - chunks + 1 - 2 * z
+        fd = s - chunks + 1 - 2 * (last - z)
 
         @pl.when((z > 0) & (z < last) & (fu >= 0) & (fu < chunks))
         def _():
@@ -384,7 +384,7 @@
 
         return 0
 
-    lax.fori_loop(0, 2 * chunks - 3 + 2 * (last - 1), step, 0)
+    lax.fori_loop(0, 2 * chunks - 1 + 2 * (last - 1), step, 0)
 
     @pl.when(is_mid)
     def _():

time: 77.6 us -> 75.7 us (0.976)
  Pallas kernels: 75.6 us -> 73.7 us
    pallas_call x1, Pallas kernels: 75.6 us -> 73.7 us  [local(): pl.pallas_call(functools.partial(kernel, n_ctx, n_ch, rows, chunks), out_...]
where the time goes in v2:
time: 75.7 us; the launch traced here: 75.5 us
  Pallas kernels  73.7 us (97%)
  local copies, waits for them, and re-layouts  1.82 us (2%)
    pallas_call x1, Pallas kernels, local(): pl.pallas_call(functools.partial(kernel, n_ctx, n_ch, rows, chunks), out_...  73.7 us
    unnamed x1, local copies, waits for them, and re-layouts  1.82 us

profile of v2, /device:TPU:0, one launch (start us, length us, event | category | flops | bytes accessed | tf_op | source)
XLA Modules:
  0.0 75.5 jit_solution(6245392805916341110)
XLA Ops:
  0.0 73.7 %hyena.1 = bf16[224,1024]{1,0:T(8,128)(2,1)} custom-call(bf16[224,1024]{1,0:T(8,128)(2,1)} %tok_ref.1, bf16[1024]{0:T(1024)(128)(2,1)} %gain_ref.1, bf16[3,1024,2048]{2,1,0:T(8,128)(2,1)} %bitcast.4, f32[3,3,512]{2,1,0:T(4,128)} %sf_ref.1, f32[16,512]{1,0:T(8,128)} %bitcast.5, f32[16,512]{1,0:T(8,128)} %bitcast.6, f32[1,512]{1,0:T(1,128)} %bitcast.7, ...), custom_call_target="tpu_custom_call" | custom-call | tf_op jit(solution)/shard_map/hyena/pallas_call | solution.py:455
  73.7 1.8 %copy.10 = bf16[224,1024]{1,0:T(8,128)(2,1)} copy(bf16[224,1024]{1,0:T(8,128)(2,1)} %hyena.1) | data formatting | bytes 917504
